TPU v7x, 256 devices: a whole 4x4x8 slice. The times are simulated.
256 devices in a mesh: dp: 32 (over x_lo, z, core), expert: 8 (over x_hi, y).
Axes of the slice: x: 4 (x_hi: 2, x_lo: 2; x = x_hi * 2 + x_lo), y: 4, z: 8, core: 2. Of those that a mesh axis runs over, the one named last changes fastest.
Arguments:
- tokens: bfloat16 [49152, 4096], P(('dp', 'expert')), may hold values from -24 to 24
- routes: int32 [49152, 2], P(('dp', 'expert')), may hold values from 0 to 7, all different within a row; in each aligned block of 192 rows (0 to 191, 192 to 383, ...) at most 64 rows name the same one
- positives: int32 [512], P(('dp', 'expert')), may hold values from 0 to 511, each once
- expert_out: bfloat16 [32, 8, 8, 64, 4096], P('dp', 'expert'), may hold values from -6 to 6
- router: bfloat16 [4096, 8], replicated, may hold values from -0.09375 to 0.09375
- norm_gain: float32 [4096], replicated, may hold values from 0.25 to 1.75
- loss_scale: float32 [], replicated, may hold values from 8192 to 65536
Outputs:
- token_grad: bfloat16 [49152, 4096], P(('dp', 'expert'))
- expert_grad: bfloat16 [32, 8, 8, 64, 4096], P('dp', 'expert')
- router_grad: float32 [4096, 8], replicated
- loss: float32 [], replicated
Inputs may be any that keep to these rules, and one draw needn't show every extreme that they name: `routes`: each row names 2 different experts; among the rows of one device no expert is named by more than 64 rows, a bound that some block reaches. `positives`: A permutation of the records.
All inputs are finite; a program needn't handle non-finite values.
Results may differ from a plain program's by a relative error of at most 0.0061.
Values may be sent and summed in bfloat16 or wider, within the bound.
No kernel may reach another device: no remote copies, remote signals or barrier semaphores. Data moves between devices by JAX's collectives and lax.ppermute only.
A program may use at most 128 MiB of HBM per device.

v0:
```python
import math
import jax
import jax.numpy as jnp
from jax import lax
from jax.sharding import PartitionSpec as P

PAIR_DEV = 2
SEQ = 48
norm_eps = 1e-05


def slot_where(routes, experts, capacity):
    hit_table = (routes[:, :, None] == jnp.arange(experts, dtype=jnp.int32)[None, None, :]).astype(
        jnp.int32
    )
    flat_hits = hit_table.reshape(-1, experts)
    before = jnp.cumsum(flat_hits, axis=0) - flat_hits
    slot_rank = jnp.sum(before * flat_hits, axis=1).reshape(routes.shape)
    return routes * capacity + slot_rank


def forward_rows(tokens, routes, received, router, norm_gain):
    experts = received.shape[0]
    capacity = received.shape[1]
    hidden_width = received.shape[2]
    logits = jnp.dot(tokens, router, preferred_element_type=jnp.float32)
    one_hot = (routes[:, :, None] == jnp.arange(experts, dtype=jnp.int32)[None, None, :]).astype(
        jnp.float32
    )
    chosen = jnp.sum(one_hot * logits[:, None, :], axis=2)
    gate_mix = jax.nn.softmax(chosen, axis=1)
    slot_rows = slot_where(routes, experts, capacity)
    fetched = received.reshape(experts * capacity, hidden_width)[slot_rows]
    summed_rows = (
        tokens.astype(jnp.float32)
        + gate_mix[:, 0:1] * fetched[:, 0].astype(jnp.float32)
        + gate_mix[:, 1:2] * fetched[:, 1].astype(jnp.float32)
    )
    inverse = lax.rsqrt(jnp.mean(summed_rows * summed_rows, axis=1, keepdims=True) + norm_eps)
    normed = summed_rows * inverse * norm_gain
    pooled = jnp.mean(normed.reshape(-1, SEQ, hidden_width), axis=1).astype(jnp.bfloat16)
    return (pooled, (gate_mix, one_hot, slot_rows, fetched, summed_rows, inverse))


def backward_rows(tokens, router, norm_gain, saved, grad_pool, experts, capacity):
    gate_mix, one_hot, slot_rows, fetched, summed_rows, inverse = saved
    hidden_width = tokens.shape[1]
    grad_rows = jnp.broadcast_to(
        grad_pool[:, None, :] / SEQ, (grad_pool.shape[0], SEQ, hidden_width)
    ).reshape(-1, hidden_width)
    weighted = grad_rows * norm_gain
    grad_summed = inverse * weighted - summed_rows * inverse**3 * jnp.mean(
        weighted * summed_rows, axis=1, keepdims=True
    )
    grad_gate = jnp.sum(grad_summed[:, None, :] * fetched.astype(jnp.float32), axis=2)
    grad_chosen = gate_mix * (grad_gate - jnp.sum(gate_mix * grad_gate, axis=1, keepdims=True))
    grad_logits = jnp.sum(one_hot * grad_chosen[:, :, None], axis=1).astype(jnp.bfloat16)
    router_part = lax.dot_general(
        tokens, grad_logits, (((0,), (0,)), ((), ())), preferred_element_type=jnp.float32
    )
    through_router = lax.dot_general(
        grad_logits, router, (((1,), (1,)), ((), ())), preferred_element_type=jnp.float32
    )
    token_grad = (grad_summed + through_router).astype(jnp.bfloat16)
    outgoing = (
        (gate_mix[:, :, None] * grad_summed[:, None, :])
        .astype(jnp.bfloat16)
        .reshape(-1, hidden_width)
    )
    sendback = (
        jnp.zeros((experts * capacity, hidden_width), jnp.bfloat16)
        .at[slot_rows.reshape(-1)]
        .set(outgoing)
    )
    return (token_grad, sendback.reshape(experts, capacity, hidden_width), router_part)


def score_rows(queries, records_all, positives, loss_scale, pair_total, score_scale):
    scores = (
        lax.dot_general(
            queries, records_all, (((1,), (1,)), ((), ())), preferred_element_type=jnp.float32
        )
        * score_scale
    )
    highest = jnp.max(scores, axis=1, keepdims=True)
    log_total = highest[:, 0] + jnp.log(jnp.sum(jnp.exp(scores - highest), axis=1))
    is_positive = jnp.arange(pair_total, dtype=jnp.int32)[None, :] == positives[:, None]
    positive_score = jnp.sum(jnp.where(is_positive, scores, jnp.zeros_like(scores)), axis=1)
    row_loss = log_total - positive_score
    softmax_rows = jnp.exp(scores - log_total[:, None])
    score_grad = (
        (softmax_rows - is_positive.astype(jnp.float32)) * (loss_scale / pair_total)
    ).astype(jnp.bfloat16)
    return (row_loss, score_grad)


def shards(tokens, routes, positives, expert_out, router, norm_gain, loss_scale):
    experts = expert_out.shape[2]
    capacity = expert_out.shape[3]
    hidden_width = expert_out.shape[4]
    received = lax.all_to_all(
        expert_out.reshape(experts, capacity, hidden_width),
        "expert",
        split_axis=0,
        concat_axis=0,
        tiled=True,
    )
    pooled, saved = forward_rows(tokens, routes, received, router, norm_gain)
    queries = pooled[:PAIR_DEV]
    records = pooled[PAIR_DEV:]
    loop_size = lax.axis_size("dp")
    column_size = lax.axis_size("expert")
    device_count = loop_size * column_size
    pair_total = PAIR_DEV * device_count
    score_scale = 4.0 / math.sqrt(hidden_width)
    records_all = lax.all_gather(records, ("dp", "expert"), axis=0, tiled=True)
    row_loss, score_grad = score_rows(
        queries, records_all, positives, loss_scale, pair_total, score_scale
    )
    loss_local = jnp.sum(row_loss)
    grad_queries = (
        jnp.dot(score_grad, records_all, preferred_element_type=jnp.float32) * score_scale
    )
    grad_records = lax.psum_scatter(
        lax.dot_general(
            score_grad, queries, (((0,), (0,)), ((), ())), preferred_element_type=jnp.float32
        )
        * score_scale,
        ("dp", "expert"),
        scatter_dimension=0,
        tiled=True,
    )
    grad_pool = jnp.concatenate([grad_queries, grad_records], axis=0)
    token_grad, sendback, router_part = backward_rows(
        tokens, router, norm_gain, saved, grad_pool, experts, capacity
    )
    returned = lax.all_to_all(sendback, "expert", split_axis=0, concat_axis=0, tiled=True)
    router_grad, loss_total = lax.psum((router_part, loss_local), ("dp", "expert"))
    expert_grad = returned.reshape(1, 1, experts, capacity, hidden_width)
    return (token_grad, expert_grad, router_grad, loss_total / pair_total)


def solution(mesh):
    placed = (
        P(("dp", "expert"), None),
        P(("dp", "expert"), None),
        P(("dp", "expert")),
        P("dp", "expert", None, None, None),
        P(),
        P(),
        P(),
    )
    return jax.shard_map(
        shards,
        mesh=mesh,
        in_specs=placed,
        out_specs=(P(("dp", "expert"), None), P("dp", "expert", None, None, None), P(), P()),
        check_vma=False,
    )
```

profile of v0, /device:TPU:8, one launch (start us, length us, event | category | flops | bytes accessed | tf_op | source)
XLA Modules:
  0.0 1506.5 jit_solution(1943185011051784695)
XLA Ops:
  7.2 0.0 copy-start
  7.2 0.0 copy-start.8
  7.2 0.0 copy-start.4
  7.2 7.5 all-to-all-start
  14.7 0.0 all-gather.3.cloned.1.call-start
  14.7 0.1 copy.45
  14.9 0.1 eq.59
  15.0 0.1 eq.55
  15.2 0.9 reduce-window.6
  16.0 0.2 slice_reduce_fusion
  16.3 0.1 fusion.7
  16.4 0.1 reshape.211
  16.5 0.1 copy.47
  16.6 0.1 copy.48
  16.8 0.1 reshape.221
  16.9 0.0 copy-done
  16.9 0.0 copy-done.4
  16.9 0.5 fusion.20
  17.5 45.7 %all-to-all-done = bf16[8,64,4096]{2,1,0:T(8,128)(2,1)} async-done(((bf16[8,64,4096]{2,1,0:T(8,128)(2,1)}), bf16[8,64,4096]{2,1,0:T(8,128)(2,1)}, u32[]{:S(2)}, u32[]{:S(2)}) %all-to-all-start) | async-done | bytes 4194336 | tf_op jit(solution)/shard_map/all_to_all | solution.py:101
  63.2 11.0 gather_fusion
  74.2 4.6 reshape.220
  78.8 0.0 copy-start.5
  78.8 7.0 fusion.17
  85.8 0.0 copy-start.6
  85.8 4.0 multiply_reduce_fusion.2
  89.9 2.4 multiply_multiply_fusion
  92.3 0.2 copy-done.2
  92.5 2.2 reduce_sum.112
  94.7 0.6 slice_bitcast_fusion
  95.3 0.0 all-gather.3.cloned.1.call-update
  95.3 0.2 all-reduce.6.cloned.1.call-start
  96.2 680.8 %all-gather.3.cloned.1.call-done = bf16[256,2,4096]{2,1,0:T(2,128)(2,1)} async-done(((bf16[1,2,4096]{2,1,0:T(2,128)(2,1)}), bf16[256,2,4096]{2,1,0:T(2,128)(2,1)}) %all-gather.3.cloned.1.call-update) | async-done | bytes 4194320 | tf_op jit(solution)/shard_map/all_gather | solution.py:116
  777.0 7.2 reshape.238
  784.2 3.5 fusion.19
  787.7 0.2 select_reduce_fusion.2
  787.9 0.6 subtract_reduce_fusion
  788.5 4.6 convolution_multiply_fusion
  793.1 0.0 all-reduce.6.cloned.1.call-update
  793.1 0.1 copy.54
  793.3 0.1 div.48
  793.4 0.1 copy.53
  793.5 0.1 reshape.214
  793.7 2.9 convolution_multiply_fusion.1
  796.6 301.1 %all-reduce.6.cloned.1.call-done = f32[512,4096]{1,0:T(8,128)} async-done(((f32[512,4096]{1,0:T(8,128)}), f32[512,4096]{1,0:T(8,128)}) %all-reduce.6.cloned.1.call-update) | async-done | bytes 8388624
  1097.7 1.1 constant_dynamic-slice_fusion
  1098.8 0.3 bitcast_multiply_fusion
  1099.2 0.5 copy-done.3
  1099.7 0.4 multiply_reduce_fusion.1
  1100.1 0.7 multiply_subtract_fusion
  1100.8 1.7 copy-done.1
  1102.5 5.3 mul.182
  1107.8 8.4 mul.189
  1116.2 9.7 scatter_custom_fusion
  1125.9 6.8 all-to-all-start.1
  1132.6 112.4 %psum.15 = f32[]{:T(128)} all-reduce(f32[]{:T(128)} %get-tuple-element.6), channel_id=1, replica_groups=mesh['dp'=32,'expert'=8] {'dp','expert'}, use_global_device_ids=true, to_apply=%region_19.20 | all-reduce | flops 1 | bytes 8 | tf_op jit(solution)/shard_map/psum | solution.py:138
  1245.7 5.7 multiply_reduce_fusion
  1251.4 0.1 copy.52
  1251.5 2.4 convolution_bitcast_fusion
  1253.9 0.0 all-reduce.4.cloned.1.call-update
  1254.0 3.6 fusion
  1257.6 0.0 all-to-all-done.1
  1257.6 235.8 %all-reduce.4.cloned.1.call-done = f32[4096,8]{0,1:T(8,128)} async-done(((f32[4096,8]{0,1:T(8,128)}), f32[4096,8]{0,1:T(8,128)}) %all-reduce.4.cloned.1.call-update) | async-done | bytes 131088 | tf_op jit(solution)/shard_map/psum | solution.py:138
  1493.4 4.7 copy.69
  1498.2 0.7 copy.70
  (28 shorter events, 0.3 us)
Async XLA Ops:
  7.2 9.7 copy-start
  7.2 7.5 copy-start.8
  7.2 9.7 copy-start.4
  7.2 56.0 %all-to-all-start = ((bf16[8,64,4096]{2,1,0:T(8,128)(2,1)}), bf16[8,64,4096]{2,1,0:T(8,128)(2,1)}, u32[]{:S(2)}, u32[]{:S(2)}) async-start(bf16[8,64,4096]{2,1,0:T(8,128)(2,1)} %bitcast.46), calls=%async_computation | async-start | bytes 8388608 | tf_op jit(solution)/shard_map/all_to_all | solution.py:101
  14.7 762.3 %all-gather.3.cloned.1.call-start = ((), (), s32[]{:S(2)}) async-start(), calls=%async_computation.3 | async-start | bytes 4210688 | tf_op jit(solution)/shard_map/all_gather | solution.py:116
  78.8 7.0 copy-start.5
  85.8 4.1 copy-start.6
  89.8 2.6 copy-start.2
  95.3 1002.4 %all-reduce.6.cloned.1.call-start = ((), (), s32[]{:S(2)}) async-start(), calls=%async_computation.4 | async-start | bytes 16777216
  784.2 3.5 copy-start.9
  1097.7 2.0 copy-start.3
  1100.8 1.7 copy-start.1
  1125.9 131.7 %all-to-all-start.1 = ((bf16[8,64,4096]{2,1,0:T(8,128)(2,1)}), bf16[8,64,4096]{2,1,0:T(8,128)(2,1)}, u32[]{:S(2)}, u32[]{:S(2)}) async-start(bf16[8,64,4096]{2,1,0:T(8,128)(2,1)} %bitcast.44), calls=%async_computation.1 | async-start | bytes 8388608 | tf_op jit(solution)/shard_map/all_to_all | solution.py:137
  1132.6 360.8 %all-reduce.4.cloned.1.call-start = ((), (), s32[]{:S(2)}) async-start(), calls=%async_computation.2 | async-start | bytes 262144 | tf_op jit(solution)/shard_map/psum | solution.py:138
  1493.4 4.7 copy-start.7
Sparse Core Ops, SparseCore 0:
  95.4 681.5 all-gather.2
  793.3 304.4 all-reduce.5
  1254.1 239.3 all-reduce.3
where the time goes:
time: 1510 us
  waiting for transfers between devices  1260 us (83%)
  blocking collectives  112 us (7%)
  local copies, waits for them, and re-layouts  54.7 us (4%)
  other arithmetic  27.5 us (2%)
  matrix products  17.5 us (1%)
  between operations  16.5 us (1%)
    all_gather x1, waiting for transfers between devices, shards(): records_all = lax.all_gather(records, ('dp', 'expert'), axis=0, tiled=True)  681 us
    unnamed x4, waiting for transfers between devices  301 us
    psum x1, waiting for transfers between devices, shards(): lax.psum((router_part, loss_local), ('dp', 'expert'))  236 us
    psum x1, blocking collectives, shards(): lax.psum((router_part, loss_local), ('dp', 'expert'))  112 us
    all_to_all x1, waiting for transfers between devices, shards(): lax.all_to_all(expert_out.reshape(experts, capacity, hidden_width), 'expe...  45.7 us
  transfers between devices with their start and end apart: 5, of which 4 were waited for; matrix products, arithmetic and copies ran while one was open for 1% of the time, Pallas kernels for 0%

commit v1 on v0

--- a/solution.py
+++ b/solution.py
@@ -1,3 +1,4 @@
+import functools
 import math
 import jax
 import jax.numpy as jnp
@@ -7,6 +8,14 @@
 PAIR_DEV = 2
 SEQ = 48
 norm_eps = 1e-05
+
+
+def store_the_sector(q_in, across, net_axis):
+    local_part = lax.psum(q_in, across)
+    return lax.psum(local_part, net_axis)
+
+
+note_strings = functools.partial(store_the_sector, across="dp", net_axis="expert")
 
 
 def slot_where(routes, experts, capacity):
@@ -135,7 +144,7 @@
         tokens, router, norm_gain, saved, grad_pool, experts, capacity
     )
     returned = lax.all_to_all(sendback, "expert", split_axis=0, concat_axis=0, tiled=True)
-    router_grad, loss_total = lax.psum((router_part, loss_local), ("dp", "expert"))
+    router_grad, loss_total = note_strings((router_part, loss_local))
     expert_grad = returned.reshape(1, 1, experts, capacity, hidden_width)
     return (token_grad, expert_grad, router_grad, loss_total / pair_total)
 

time: 1510 us -> 1440 us (0.954)
  blocking collectives: 112 us -> 78.1 us
  waiting for transfers between devices: 1260 us -> 1230 us
    psum x1 -> x2, blocking collectives: 112 us -> 78.1 us  [the longest x1 56.6 us: store_the_sector(): local_part = lax.psum(q_in, across)]
    psum x1 -> x2, waiting for transfers between devices: 236 us -> 203 us  [the longest x1 120 us: store_the_sector(): local_part = lax.psum(q_in, across)]
    unnamed x4 -> x5, waiting for transfers between devices: 301 us -> 301 us
  transfers between devices with their start and end apart: 5 -> 6, of which waited for: 4 -> 5; matrix products, arithmetic and copies ran while one was open for 1% -> 1% of each run, Pallas kernels for 0% -> 0%
where the time goes in v1:
time: 1440 us
  waiting for transfers between devices  1230 us (85%)
  blocking collectives  78.1 us (5%)
  local copies, waits for them, and re-layouts  54.7 us (4%)
  other arithmetic  27.5 us (2%)
  matrix products  17.5 us (1%)
  between operations  16.5 us (1%)
  starting transfers between devices  14.6 us (1%)
    all_gather x1, waiting for transfers between devices, shards(): records_all = lax.all_gather(records, ('dp', 'expert'), axis=0, tiled=True)  681 us
    unnamed x5, waiting for transfers between devices  301 us
    psum x1, waiting for transfers between devices, store_the_sector(): local_part = lax.psum(q_in, across)  120 us
    psum x1, waiting for transfers between devices, store_the_sector(): return lax.psum(local_part, net_axis)  83 us
    psum x1, blocking collectives, store_the_sector(): local_part = lax.psum(q_in, across)  56.6 us
    all_to_all x1, waiting for transfers between devices, shards(): lax.all_to_all(expert_out.reshape(experts, capacity, hidden_width), 'expe...  45.7 us
  transfers between devices with their start and end apart: 6, of which 5 were waited for; matrix products, arithmetic and copies ran while one was open for 1% of the time, Pallas kernels for 0%

profile of v1, /device:TPU:8, one launch (start us, length us, event | category | flops | bytes accessed | tf_op | source)
XLA Modules:
  0.0 1439.9 jit_solution(11954634948594039915)
XLA Ops:
  7.2 0.0 copy-start
  7.2 0.0 copy-start.4
  7.2 7.5 all-to-all-start
  14.7 0.1 copy.45
  14.9 0.1 eq.59
  15.0 0.1 eq.55
  15.2 0.9 reduce-window.6
  16.0 0.2 slice_reduce_fusion
  16.3 0.1 fusion.7
  16.4 0.1 reshape.211
  16.5 0.1 copy.47
  16.6 0.1 copy.48
  16.7 0.1 reshape.221
  16.9 0.5 fusion.20
  17.5 45.7 %all-to-all-done = bf16[8,64,4096]{2,1,0:T(8,128)(2,1)} async-done(((bf16[8,64,4096]{2,1,0:T(8,128)(2,1)}), bf16[8,64,4096]{2,1,0:T(8,128)(2,1)}, u32[]{:S(2)}, u32[]{:S(2)}) %all-to-all-start) | async-done | bytes 4194336 | tf_op jit(solution)/shard_map/all_to_all | solution.py:110
  63.2 11.0 gather_fusion
  74.2 4.6 reshape.220
  78.8 0.0 copy-start.5
  78.8 7.0 fusion.17
  85.8 0.0 copy-start.6
  85.8 4.0 multiply_reduce_fusion.2
  89.9 2.4 multiply_multiply_fusion
  92.3 0.2 copy-done.2
  92.5 2.2 reduce_sum.112
  94.7 0.6 slice_bitcast_fusion
  95.3 0.0 all-gather.3.cloned.1.call-update
  95.3 0.2 all-reduce.9.cloned.1.call-start
  96.2 680.8 %all-gather.3.cloned.1.call-done = bf16[256,2,4096]{2,1,0:T(2,128)(2,1)} async-done(((bf16[1,2,4096]{2,1,0:T(2,128)(2,1)}), bf16[256,2,4096]{2,1,0:T(2,128)(2,1)}) %all-gather.3.cloned.1.call-update) | async-done | bytes 4194320 | tf_op jit(solution)/shard_map/all_gather | solution.py:125
  777.0 7.2 reshape.238
  784.2 3.5 fusion.19
  787.7 0.2 select_reduce_fusion.2
  787.9 0.6 subtract_reduce_fusion
  788.5 4.6 convolution_multiply_fusion
  793.1 0.0 all-reduce.9.cloned.1.call-update
  793.1 0.1 copy.54
  793.3 0.1 div.48
  793.4 0.1 copy.53
  793.5 0.1 reshape.214
  793.7 2.9 convolution_multiply_fusion.1
  796.6 301.1 %all-reduce.9.cloned.1.call-done = f32[512,4096]{1,0:T(8,128)} async-done(((f32[512,4096]{1,0:T(8,128)}), f32[512,4096]{1,0:T(8,128)}) %all-reduce.9.cloned.1.call-update) | async-done | bytes 8388624
  1097.7 1.1 constant_dynamic-slice_fusion
  1098.8 0.3 bitcast_multiply_fusion
  1099.2 0.5 copy-done.3
  1099.7 0.4 multiply_reduce_fusion.1
  1100.1 0.7 multiply_subtract_fusion
  1100.8 1.7 copy-done.1
  1102.5 5.3 mul.182
  1107.8 8.4 mul.189
  1116.2 9.7 scatter_custom_fusion
  1125.9 6.8 all-to-all-start.1
  1132.6 5.7 multiply_reduce_fusion
  1138.4 0.1 copy.52
  1138.5 2.4 convolution_bitcast_fusion
  1140.9 0.0 all-reduce.5.cloned.1.call-update
  1140.9 0.0 all-reduce.7.cloned.1.call-start
  1141.0 56.6 %psum.30 = f32[]{:T(128)} all-reduce(f32[]{:T(128)} %get-tuple-element.6), channel_id=1, replica_groups=mesh['dp'=32,'expert'=8] {'dp'}, use_global_device_ids=true, to_apply=%region_20.21 | all-reduce | flops 1 | bytes 8 | tf_op jit(solution)/shard_map/psum | solution.py:14
  1197.5 21.5 %psum.31 = f32[]{:T(128)} all-reduce(f32[]{:T(128)} %psum.30), channel_id=1, replica_groups=mesh['dp'=32,'expert'=8] {'expert'}, use_global_device_ids=true, to_apply=%region_21.22 | all-reduce | flops 1 | bytes 8 | tf_op jit(solution)/shard_map/psum | solution.py:15
  1219.7 120.5 %all-reduce.5.cloned.1.call-done = f32[4096,8]{0,1:T(8,128)} async-done(((f32[4096,8]{0,1:T(8,128)}), f32[4096,8]{0,1:T(8,128)}) %all-reduce.5.cloned.1.call-update) | async-done | bytes 131088 | tf_op jit(solution)/shard_map/psum | solution.py:14
  1340.2 0.0 all-reduce.7.cloned.1.call-update
  1340.2 3.6 fusion
  1343.9 0.0 all-to-all-done.1
  1343.9 83.0 %all-reduce.7.cloned.1.call-done = f32[4096,8]{0,1:T(8,128)} async-done(((f32[4096,8]{0,1:T(8,128)}), f32[4096,8]{0,1:T(8,128)}) %all-reduce.7.cloned.1.call-update) | async-done | bytes 131088 | tf_op jit(solution)/shard_map/psum | solution.py:15
  1426.8 4.7 copy.70
  1431.6 0.7 copy.71
  (32 shorter events, 0.3 us)
Async XLA Ops:
  7.2 9.7 copy-start
  7.2 7.5 copy-start.8
  7.2 9.7 copy-start.4
  7.2 56.0 %all-to-all-start = ((bf16[8,64,4096]{2,1,0:T(8,128)(2,1)}), bf16[8,64,4096]{2,1,0:T(8,128)(2,1)}, u32[]{:S(2)}, u32[]{:S(2)}) async-start(bf16[8,64,4096]{2,1,0:T(8,128)(2,1)} %bitcast.46), calls=%async_computation | async-start | bytes 8388608 | tf_op jit(solution)/shard_map/all_to_all | solution.py:110
  14.7 762.3 %all-gather.3.cloned.1.call-start = ((), (), s32[]{:S(2)}) async-start(), calls=%async_computation.4 | async-start | bytes 4210688 | tf_op jit(solution)/shard_map/all_gather | solution.py:125
  78.8 7.0 copy-start.5
  85.8 4.1 copy-start.6
  89.8 2.6 copy-start.2
  95.3 1002.4 %all-reduce.9.cloned.1.call-start = ((), (), s32[]{:S(2)}) async-start(), calls=%async_computation.5 | async-start | bytes 16777216
  784.2 3.5 copy-start.9
  1097.7 2.0 copy-start.3
  1100.8 1.7 copy-start.1
  1125.9 218.0 %all-to-all-start.1 = ((bf16[8,64,4096]{2,1,0:T(8,128)(2,1)}), bf16[8,64,4096]{2,1,0:T(8,128)(2,1)}, u32[]{:S(2)}, u32[]{:S(2)}) async-start(bf16[8,64,4096]{2,1,0:T(8,128)(2,1)} %bitcast.44), calls=%async_computation.1 | async-start | bytes 8388608 | tf_op jit(solution)/shard_map/all_to_all | solution.py:146
  1132.6 207.5 %all-reduce.5.cloned.1.call-start = ((), (), s32[]{:S(2)}) async-start(), calls=%async_computation.2 | async-start | bytes 262144 | tf_op jit(solution)/shard_map/psum | solution.py:14
  1140.9 285.9 %all-reduce.7.cloned.1.call-start = ((), (), s32[]{:S(2)}) async-start(), calls=%async_computation.3 | async-start | bytes 262144 | tf_op jit(solution)/shard_map/psum | solution.py:15
  1426.8 4.7 copy-start.7
Sparse Core Ops, SparseCore 0:
  95.4 681.5 all-gather.2
  793.3 304.4 all-reduce.8
  1141.0 199.0 all-reduce.4
  1342.6 84.1 all-reduce.6
